TPU v7x, 32 devices: a whole 2x2x4 slice. The times are simulated.
32 devices in a mesh: fsdp: 8 (over z, x), tensor: 2 (over y), dp: 2 (over core).
Axes of the slice: x: 2, y: 2, z: 4, core: 2. Of those that a mesh axis runs over, the one named last changes fastest.
Arguments:
- states: bfloat16 [4096, 4096], P('fsdp', ('tensor', 'dp')), may hold values from -6 to 6
- fresh_rows: bfloat16 [4096, 4096], P('fsdp', ('tensor', 'dp')), may hold values from -6 to 6
- norm_gain: bfloat16 [4096], P(('tensor', 'dp')), may hold values from 0.25 to 1.75
- gate_weight: bfloat16 [4096, 8192], P('fsdp', ('tensor', 'dp')), may hold values from -0.09375 to 0.09375
- up_weight: bfloat16 [4096, 8192], P('fsdp', ('tensor', 'dp')), may hold values from -0.09375 to 0.09375
- down_weight: bfloat16 [8192, 4096], P(('tensor', 'dp'), 'fsdp'), may hold values from -0.09375 to 0.09375
- halted: int32 [64, 64], P('fsdp'), may hold values from 0 to 1, as said below
- refill_index: int32 [64, 64], P('fsdp'), may hold values from 0 to 63, each once within a row
Outputs:
- next_states: bfloat16 [4096, 4096], P('fsdp', ('tensor', 'dp'))
Inputs may be any that keep to these rules, and one draw needn't show every extreme that they name: In each aligned block of 512 rows (in row order over all batches) at most 384 rows are running (halted 0), and some block has exactly 384 running rows. Each batch's row of refill_index holds every number of 0 to 63 once.
All inputs are finite; a program needn't handle non-finite values.
Results may differ from a plain program's by a relative error of at most 0.0085.
Values may be sent and summed in bfloat16 or wider, within the bound.
A program may use at most 128 MiB of HBM per device.

v0:
```python
import jax
import jax.numpy as jnp
from jax import lax
from jax.sharding import PartitionSpec as P

norm_eps = 1e-05


def block_update(source, norm_gain, gate_weight, up_weight, down_weight):
    gathered, gain_full = (
        lax.all_gather(source, ("tensor", "dp"), axis=1, tiled=True),
        lax.all_gather(norm_gain, ("tensor", "dp"), axis=0, tiled=True),
    )
    widened = gathered.astype(jnp.float32)
    mean_square = jnp.mean(widened * widened, axis=-1, keepdims=True)
    normed = (widened * lax.rsqrt(mean_square + norm_eps) * gain_full.astype(jnp.float32)).astype(
        jnp.bfloat16
    )
    gate_more = jnp.dot(
        normed,
        lax.all_gather(gate_weight, "fsdp", axis=0, tiled=True),
        preferred_element_type=jnp.float32,
    )
    up_more = jnp.dot(
        normed,
        lax.all_gather(up_weight, "fsdp", axis=0, tiled=True),
        preferred_element_type=jnp.float32,
    )
    hidden = (jax.nn.silu(gate_more) * up_more).astype(jnp.bfloat16)
    partial_value = jnp.dot(
        hidden,
        lax.all_gather(down_weight, "fsdp", axis=1, tiled=True),
        preferred_element_type=jnp.float32,
    )
    return lax.psum_scatter(
        partial_value.astype(jnp.bfloat16), ("tensor", "dp"), scatter_dimension=1, tiled=True
    ).astype(jnp.float32)


def body(states, fresh_rows, norm_gain, gate_weight, up_weight, down_weight, halted, refill_index):
    row_count = states.shape[0]
    running = halted.reshape(row_count) == 0
    capacity = row_count * 3 // 4
    slot_of = jnp.cumsum(running.astype(jnp.int32)) - 1
    slot_ids = lax.iota(jnp.int32, capacity)
    picker = ((slot_of[None, :] == slot_ids[:, None]) & running[None, :]).astype(jnp.bfloat16)
    source = jnp.dot(picker, states, preferred_element_type=jnp.float32).astype(jnp.bfloat16)
    compact = block_update(source, norm_gain, gate_weight, up_weight, down_weight)
    update = jnp.take(compact, jnp.clip(slot_of, 0, capacity - 1), axis=0)
    block_total = refill_index.shape[0]
    batch_len = refill_index.shape[1]
    fresh_blocks = fresh_rows.reshape(block_total, batch_len, fresh_rows.shape[1])
    refilled = jax.vmap(lambda block_rows, pick_index: block_rows[pick_index])(
        fresh_blocks, refill_index
    )
    refilled = refilled.reshape(row_count, fresh_rows.shape[1])
    computed = (states.astype(jnp.float32) + update).astype(jnp.bfloat16)
    return jnp.where(running[:, None], computed, refilled)


def solution(mesh):
    in_specs = (
        P("fsdp", ("tensor", "dp")),
        P("fsdp", ("tensor", "dp")),
        P(("tensor", "dp")),
        P("fsdp", ("tensor", "dp")),
        P("fsdp", ("tensor", "dp")),
        P(("tensor", "dp"), "fsdp"),
        P("fsdp", None),
        P("fsdp", None),
    )
    out_specs = P("fsdp", ("tensor", "dp"))
    return jax.shard_map(body, mesh=mesh, in_specs=in_specs, out_specs=out_specs, check_vma=False)
```

profile of v0, /device:TPU:0, one launch (start us, length us, event | category | flops | bytes accessed | tf_op | source)
XLA Modules:
  0.0 803.4 jit_solution(10444308348933228802)
XLA Ops:
  6.5 0.0 copy-start
  6.5 0.0 all-gather.5.cloned.1.call-start
  6.5 0.8 fusion.21
  7.3 0.1 reshape.107
  7.4 0.3 reduce-window.9
  7.7 0.1 slice.7
  7.8 0.1 slice_reduce_fusion
  7.9 0.1 compare_and_fusion
  8.0 0.1 eq.40
  8.1 2.7 convolution_convert_fusion.1
  10.8 0.0 all-gather.5.cloned.1.call-update
  10.8 0.0 copy-start.2
  10.8 0.0 all-gather.7.cloned.1.call-start
  10.9 0.7 all-gather.7.cloned.1.call-update
  11.6 0.0 all-gather.11.cloned.1.call-start
  11.6 0.7 all-gather.11.cloned.1.call-update
  12.3 0.0 all-gather.9.cloned.1.call-start
  12.4 0.5 all-gather.9.cloned.1.call-update
  12.9 0.0 reduce-scatter.2.cloned.1.call-start
  12.9 0.0 copy-done.2
  12.9 6.2 all_gather.16
  19.1 23.1 %all-gather.5.cloned.1.call-done = bf16[384,4096]{1,0:T(8,128)(2,1)} async-done(((bf16[384,1024]{1,0:T(8,128)(2,1)}), bf16[384,4096]{1,0:T(8,128)(2,1)}) %all-gather.5.cloned.1.call-update) | async-done | bytes 3145744 | tf_op jit(solution)/shard_map/all_gather | solution.py:11
  42.2 2.6 fusion
  44.8 226.8 %all-gather.7.cloned.1.call-done = bf16[4096,2048]{1,0:T(8,128)(2,1)} async-done(((bf16[512,2048]{1,0:T(8,128)(2,1)}), bf16[4096,2048]{1,0:T(8,128)(2,1)}) %all-gather.7.cloned.1.call-update) | async-done | bytes 16777232 | tf_op jit(solution)/shard_map/all_gather | solution.py:21
  271.6 12.3 %fusion.7 = f32[384,2048]{1,0:T(8,128)} fusion(bf16[4096,2048]{1,0:T(8,128)(2,1)} %all-gather.7.cloned.1.call-done, bf16[384,4096]{1,0:T(8,128)(2,1)} %all-gather.5.cloned.1.call-done, f32[4096]{0:T(1024)S(1)} %convert_element_type.40, f32[384]{0:T(512)S(1)} %add_rsqrt_fusion), kind=kOutput, calls=%fused_computation.13 | convolution fusion | flops 6448742400 | bytes 23086592 | tf_op jit(solution)/shard_map/dot_general | solution.py:19
  284.0 215.2 %all-gather.11.cloned.1.call-done = bf16[2048,4096]{1,0:T(8,128)(2,1)} async-done(((bf16[2048,512]{1,0:T(8,128)(2,1)}), bf16[2048,4096]{1,0:T(8,128)(2,1)}) %all-gather.11.cloned.1.call-update) | async-done | bytes 16777232 | tf_op jit(solution)/shard_map/all_gather | solution.py:32
  499.2 227.5 %all-gather.9.cloned.1.call-done = bf16[4096,2048]{1,0:T(8,128)(2,1)} async-done(((bf16[512,2048]{1,0:T(8,128)(2,1)}), bf16[4096,2048]{1,0:T(8,128)(2,1)}) %all-gather.9.cloned.1.call-update) | async-done | bytes 16777232 | tf_op jit(solution)/shard_map/all_gather | solution.py:26
  726.7 26.5 %convolution_convert_fusion = bf16[384,4096]{1,0:T(8,128)(2,1)} fusion(bf16[2048,4096]{1,0:T(8,128)(2,1)} %all-gather.11.cloned.1.call-done, f32[384,2048]{1,0:T(8,128)} %fusion.7, bf16[4096,2048]{1,0:T(8,128)(2,1)} %all-gather.9.cloned.1.call-done, bf16[384,4096]{1,0:T(8,128)(2,1)} %all-gather.5.cloned.1.call-done, f32[4096]{0:T(1024)S(1)} %convert_element_type.40, ...), kind=kOutput, calls=%fused_computation.7 | convolution fusion | flops 12897484800 | bytes 43009536 | tf_op jit(solution)/shard_map/dot_general | solution.py:30
  753.2 0.0 copy-start.1
  753.2 0.0 reduce-scatter.2.cloned.1.call-update
  753.2 0.7 copy-done.1
  753.9 0.1 reshape.116
  753.9 0.0 copy-done
  754.0 7.9 gather_fusion.1
  761.9 0.1 fusion.17
  762.0 27.3 %reduce-scatter.2.cloned.1.call-done = bf16[384,1024]{1,0:T(8,128)(2,1)} async-done(((bf16[384,4096]{1,0:T(8,128)(2,1)}), bf16[384,1024]{1,0:T(8,128)(2,1)}) %reduce-scatter.2.cloned.1.call-update) | async-done | bytes 786448 | tf_op jit(solution)/shard_map/reduce_scatter | solution.py:35
  789.3 1.3 convert_element_type.44
  790.6 2.7 gather_fusion
  793.3 3.6 fusion.4
  (6 shorter events, 0.1 us)
Async XLA Ops:
  6.5 747.4 %copy-start = (bf16[512,1024]{1,0:T(8,128)(2,1)S(1)}, bf16[512,1024]{1,0:T(8,128)(2,1)}, u32[]{:S(2)}) copy-start(bf16[512,1024]{1,0:T(8,128)(2,1)} %param.9) | copy-start | bytes 3145732
  6.5 35.7 %all-gather.5.cloned.1.call-start = ((), (), s32[]{:S(2)}) async-start(), calls=%async_computation.1 | async-start | bytes 3932160 | tf_op jit(solution)/shard_map/all_gather | solution.py:11
  10.8 2.1 copy-start.2
  10.8 260.8 %all-gather.7.cloned.1.call-start = ((), (), s32[]{:S(2)}) async-start(), calls=%async_computation.2 | async-start | bytes 18874368 | tf_op jit(solution)/shard_map/all_gather | solution.py:21
  11.6 487.6 %all-gather.11.cloned.1.call-start = ((), (), s32[]{:S(2)}) async-start(), calls=%async_computation.4 | async-start | bytes 18874368 | tf_op jit(solution)/shard_map/all_gather | solution.py:32
  12.3 714.4 %all-gather.9.cloned.1.call-start = ((), (), s32[]{:S(2)}) async-start(), calls=%async_computation.3 | async-start | bytes 18874368 | tf_op jit(solution)/shard_map/all_gather | solution.py:26
  12.9 776.4 %reduce-scatter.2.cloned.1.call-start = ((), (), s32[]{:S(2)}) async-start(), calls=%async_computation.5 | async-start | bytes 3932160 | tf_op jit(solution)/shard_map/reduce_scatter | solution.py:35
  753.2 0.7 copy-start.1
Sparse Core Ops, SparseCore 0:
  10.9 31.2 all-gather.4
  44.3 227.2 all-gather.6
  273.7 225.4 all-gather.10
  501.2 225.4 all-gather.8
  753.3 35.9 reduce-scatter.1
where the time goes:
time: 804 us; the launch traced here: 803 us
  waiting for transfers between devices  722 us (90%)
  matrix products  41.5 us (5%)
  between operations  13.2 us (2%)
  local copies, waits for them, and re-layouts  11.7 us (1%)
  other arithmetic  8.79 us (1%)
    all_gather x1, waiting for transfers between devices, block_update(): lax.all_gather(up_weight, 'fsdp', axis=0, tiled=True)  227 us
    all_gather x1, waiting for transfers between devices, block_update(): lax.all_gather(gate_weight, 'fsdp', axis=0, tiled=True)  227 us
    all_gather x1, waiting for transfers between devices, block_update(): lax.all_gather(down_weight, 'fsdp', axis=1, tiled=True)  215 us
    reduce_scatter x1, waiting for transfers between devices, block_update(): lax.psum_scatter(partial_value.astype(jnp.bfloat16), ('tensor', 'dp'), sc...  27.3 us
    dot_general x1, matrix products, block_update(): jnp.dot(hidden, lax.all_gather(down_weight, 'fsdp', axis=1, tiled=True),...  26.5 us
    all_gather x1, waiting for transfers between devices, block_update(): lax.all_gather(source, ('tensor', 'dp'), axis=1, tiled=True)  23.1 us
  transfers between devices with their start and end apart: 5, of which 5 were waited for; matrix products, arithmetic and copies ran while one was open for 3% of the time, Pallas kernels for 0%

commit v1 on v0

--- a/solution.py
+++ b/solution.py
@@ -4,6 +4,19 @@
 from jax.sharding import PartitionSpec as P
 
 norm_eps = 1e-05
+
+
+def collect(x, axis, dim):
+    size, mine, span = (lax.axis_size(axis), lax.axis_index(axis), x.shape[dim])
+    upward = [(i, (i + 1) % size) for i in range(size)]
+    out = jnp.zeros((*x.shape[:dim], size * span, *x.shape[dim + 1 :]), x.dtype)
+    block = x
+    for step in range(size):
+        owner = (mine - step) % size
+        out = lax.dynamic_update_slice_in_dim(out, block, owner * span, axis=dim)
+        if step < size - 1:
+            block = lax.ppermute(block, axis, upward)
+    return out
 
 
 def block_update(source, norm_gain, gate_weight, up_weight, down_weight):
@@ -16,11 +29,7 @@
     normed = (widened * lax.rsqrt(mean_square + norm_eps) * gain_full.astype(jnp.float32)).astype(
         jnp.bfloat16
     )
-    gate_more = jnp.dot(
-        normed,
-        lax.all_gather(gate_weight, "fsdp", axis=0, tiled=True),
-        preferred_element_type=jnp.float32,
-    )
+    gate_more = jnp.dot(normed, collect(gate_weight, "fsdp", 0), preferred_element_type=jnp.float32)
     up_more = jnp.dot(
         normed,
         lax.all_gather(up_weight, "fsdp", axis=0, tiled=True),

time: 804 us -> 822 us (1.022)
  local copies, waits for them, and re-layouts: 11.7 us -> 40.6 us
  waiting for transfers between devices: 722 us -> 708 us
    ppermute x0 -> x7, waiting for transfers between devices: none -> 568 us  [collect(): block = lax.ppermute(block, axis, upward)]
    all_gather x1, waiting for transfers between devices: 227 us -> 0.01 us  [block_update(): lax.all_gather(up_weight, 'fsdp', axis=0, tiled=True)]
    all_gather x1 -> x0, waiting for transfers between devices: 227 us -> none  [block_update(): lax.all_gather(gate_weight, 'fsdp', axis=0, tiled=True)]
    all_gather x1, waiting for transfers between devices: 215 us -> 110 us  [block_update(): lax.all_gather(down_weight, 'fsdp', axis=1, tiled=True)]
    all_gather x1, waiting for transfers between devices: 23.1 us -> 0.01 us  [block_update(): lax.all_gather(source, ('tensor', 'dp'), axis=1, tiled=True)]
    dynamic_update_slice x0 -> x8, local copies, waits for them, and re-layouts: none -> 17.2 us  [collect(): out = lax.dynamic_update_slice_in_dim(out, block, owner * span, axis=dim)]
  transfers between devices with their start and end apart: 5 -> 11, of which waited for: 5 -> 9; matrix products, arithmetic and copies ran while one was open for 3% -> 6% of each run, Pallas kernels for 0% -> 0%
where the time goes in v1:
time: 822 us
  waiting for transfers between devices  708 us (86%)
  matrix products  41.6 us (5%)
  local copies, waits for them, and re-layouts  40.6 us (5%)
  between operations  13.2 us (2%)
  other arithmetic  8.94 us (1%)
    ppermute x7, waiting for transfers between devices, collect(): block = lax.ppermute(block, axis, upward)  568 us
    all_gather x1, waiting for transfers between devices, block_update(): lax.all_gather(down_weight, 'fsdp', axis=1, tiled=True)  110 us
    reduce_scatter x1, waiting for transfers between devices, block_update(): lax.psum_scatter(partial_value.astype(jnp.bfloat16), ('tensor', 'dp'), sc...  28 us
    dot_general x1, matrix products, block_update(): jnp.dot(hidden, lax.all_gather(down_weight, 'fsdp', axis=1, tiled=True),...  26.3 us
    dynamic_update_slice x8, local copies, waits for them, and re-layouts, collect(): out = lax.dynamic_update_slice_in_dim(out, block, owner * span, axis=dim)  17.2 us
  transfers between devices with their start and end apart: 11, of which 9 were waited for; matrix products, arithmetic and copies ran while one was open for 6% of the time, Pallas kernels for 0%

profile of v1, /device:TPU:0, one launch (start us, length us, event | category | flops | bytes accessed | tf_op | source)
XLA Modules:
  0.0 821.6 jit_solution(4628258196972856042)
XLA Ops:
  6.5 0.8 fusion.25
  7.3 0.1 reshape.107
  7.4 0.3 reduce-window.9
  7.7 0.1 slice.7
  7.8 0.1 slice_reduce_fusion
  7.9 0.1 compare_and_fusion
  8.0 0.1 eq.49
  8.1 2.8 convolution_convert_fusion.1
  11.0 0.0 all-gather.6.cloned.1.call-start
  11.0 0.7 all-gather.6.cloned.1.call-update
  11.7 0.0 all-gather.8.cloned.1.call-start
  11.8 0.7 all-gather.8.cloned.1.call-update
  12.5 0.0 reduce-scatter.2.cloned.1.call-start
  12.5 3.0 collective-permute-start
  15.5 53.7 %collective-permute-done = bf16[512,2048]{1,0:T(8,128)(2,1)S(1)} collective-permute-done((bf16[512,2048]{1,0:T(8,128)(2,1)S(1)}, bf16[512,2048]{1,0:T(8,128)(2,1)S(1)}, u32[]{:S(2)}, u32[]{:S(2)}) %collective-permute-start) | collective-permute-done | bytes 2097184 | tf_op jit(solution)/shard_map/ppermute | solution.py:18
  69.2 0.6 collective-permute-start.1
  69.9 0.7 copy-done.4
  70.5 93.7 %collective-permute-done.1 = bf16[512,2048]{1,0:T(8,128)(2,1)S(1)} collective-permute-done((bf16[512,2048]{1,0:T(8,128)(2,1)S(1)}, bf16[512,2048]{1,0:T(8,128)(2,1)S(1)}, u32[]{:S(2)}, u32[]{:S(2)}) %collective-permute-start.1) | collective-permute-done | bytes 2097184 | tf_op jit(solution)/shard_map/ppermute | solution.py:18
  164.3 1.3 copy-done.8
  165.6 83.8 %collective-permute-done.2 = bf16[512,2048]{1,0:T(8,128)(2,1)S(1)} collective-permute-done((bf16[512,2048]{1,0:T(8,128)(2,1)S(1)}, bf16[512,2048]{1,0:T(8,128)(2,1)S(1)}, u32[]{:S(2)}, u32[]{:S(2)}) %collective-permute-start.2) | collective-permute-done | bytes 2097184 | tf_op jit(solution)/shard_map/ppermute | solution.py:18
  249.3 1.4 copy-done.2
  250.7 95.0 %collective-permute-done.3 = bf16[512,2048]{1,0:T(8,128)(2,1)S(1)} collective-permute-done((bf16[512,2048]{1,0:T(8,128)(2,1)S(1)}, bf16[512,2048]{1,0:T(8,128)(2,1)S(1)}, u32[]{:S(2)}, u32[]{:S(2)}) %collective-permute-start.3) | collective-permute-done | bytes 2097184 | tf_op jit(solution)/shard_map/ppermute | solution.py:18
  345.7 1.3 copy-done.6
  347.0 99.5 %collective-permute-done.4 = bf16[512,2048]{1,0:T(8,128)(2,1)} collective-permute-done((bf16[512,2048]{1,0:T(8,128)(2,1)S(1)}, bf16[512,2048]{1,0:T(8,128)(2,1)}, u32[]{:S(2)}, u32[]{:S(2)}) %collective-permute-start.4) | collective-permute-done | bytes 2097184 | tf_op jit(solution)/shard_map/ppermute | solution.py:18
  446.5 5.2 all_gather.13
  451.7 7.0 broadcast_in_dim.32
  458.8 1.6 constant_dynamic-update-slice_fusion.7
  460.3 71.7 %collective-permute-done.5 = bf16[512,2048]{1,0:T(8,128)(2,1)} collective-permute-done((bf16[512,2048]{1,0:T(8,128)(2,1)}, bf16[512,2048]{1,0:T(8,128)(2,1)}, u32[]{:S(2)}, u32[]{:S(2)}) %collective-permute-start.5) | collective-permute-done | bytes 2097184 | tf_op jit(solution)/shard_map/ppermute | solution.py:18
  532.0 1.5 constant_dynamic-update-slice_fusion.6
  533.5 1.5 constant_dynamic-update-slice_fusion.5
  535.0 2.7 fusion
  537.7 1.6 constant_dynamic-update-slice_fusion.4
  539.3 1.5 constant_dynamic-update-slice_fusion.3
  540.8 3.2 constant_dynamic-update-slice_fusion.2
  544.0 3.1 constant_dynamic-update-slice_fusion.1
  547.2 71.0 %collective-permute-done.6 = bf16[512,2048]{1,0:T(8,128)(2,1)} collective-permute-done((bf16[512,2048]{1,0:T(8,128)(2,1)}, bf16[512,2048]{1,0:T(8,128)(2,1)}, u32[]{:S(2)}, u32[]{:S(2)}) %collective-permute-start.6) | collective-permute-done | bytes 2097184 | tf_op jit(solution)/shard_map/ppermute | solution.py:18
  618.2 3.2 constant_dynamic-update-slice_fusion
  621.5 12.5 %fusion.5 = f32[384,2048]{1,0:T(8,128)} fusion(bf16[4096,2048]{1,0:T(8,128)(2,1)} %all-gather.6.cloned.1.call-done, bf16[384,4096]{1,0:T(8,128)(2,1)} %all-gather.4.cloned.1.call-done, f32[4096]{0:T(1024)S(1)} %convert_element_type.40, f32[384]{0:T(512)S(1)} %add_rsqrt_fusion), kind=kOutput, calls=%fused_computation.13 | convolution fusion | flops 6448742400 | bytes 23086592 | tf_op jit(solution)/shard_map/dot_general | solution.py:33
  633.9 110.5 %all-gather.8.cloned.1.call-done = bf16[2048,4096]{1,0:T(8,128)(2,1)} async-done(((bf16[2048,512]{1,0:T(8,128)(2,1)}), bf16[2048,4096]{1,0:T(8,128)(2,1)}) %all-gather.8.cloned.1.call-update) | async-done | bytes 16777232 | tf_op jit(solution)/shard_map/all_gather | solution.py:41
  744.4 26.3 %convolution_convert_fusion = bf16[384,4096]{1,0:T(8,128)(2,1)} fusion(bf16[2048,4096]{1,0:T(8,128)(2,1)} %all-gather.8.cloned.1.call-done, f32[384,2048]{1,0:T(8,128)} %fusion.5, bf16[4096,2048]{1,0:T(8,128)(2,1)} %constant_dynamic-update-slice_fusion, bf16[384,4096]{1,0:T(8,128)(2,1)} %all-gather.4.cloned.1.call-done, f32[4096]{0:T(1024)S(1)} %convert_element_type.40, ...), kind=kOutput, calls=%fused_computation.7 | convolution fusion | flops 12897484800 | bytes 43009536 | tf_op jit(solution)/shard_map/dot_general | solution.py:39
  770.7 0.7 copy-done.10
  771.4 0.1 reshape.116
  771.5 7.9 gather_fusion.1
  779.4 0.1 fusion.21
  779.5 28.0 %reduce-scatter.2.cloned.1.call-done = bf16[384,1024]{1,0:T(8,128)(2,1)} async-done(((bf16[384,4096]{1,0:T(8,128)(2,1)}), bf16[384,1024]{1,0:T(8,128)(2,1)}) %reduce-scatter.2.cloned.1.call-update) | async-done | bytes 786448 | tf_op jit(solution)/shard_map/reduce_scatter | solution.py:44
  807.5 1.3 convert_element_type.44
  808.8 2.7 gather_fusion
  811.5 3.6 fusion.4
  (35 shorter events, 0.2 us)
Async XLA Ops:
  6.5 764.9 %copy-start = (bf16[512,1024]{1,0:T(8,128)(2,1)S(1)}, bf16[512,1024]{1,0:T(8,128)(2,1)}, u32[]{:S(2)}) copy-start(bf16[512,1024]{1,0:T(8,128)(2,1)} %param.9) | copy-start | bytes 3145732
  6.5 528.5 %all-gather.4.cloned.1.call-start = ((), (), s32[]{:S(2)}) async-start(), calls=%async_computation.1 | async-start | bytes 3932160 | tf_op jit(solution)/shard_map/all_gather | solution.py:24
  8.1 4.4 copy-start.1
  10.9 435.6 %copy-start.11 = (bf16[1024]{0:T(1024)(128)(2,1)S(1)}, bf16[1024]{0:T(1024)(128)(2,1)}, u32[]{:S(2)}) copy-start(bf16[1024]{0:T(1024)(128)(2,1)} %param.10) | copy-start | bytes 6148
  11.0 610.5 %all-gather.6.cloned.1.call-start = ((), (), s32[]{:S(2)}) async-start(), calls=%async_computation.2 | async-start | bytes 18874368 | tf_op jit(solution)/shard_map/all_gather | solution.py:35
  11.7 732.7 %all-gather.8.cloned.1.call-start = ((), (), s32[]{:S(2)}) async-start(), calls=%async_computation.3 | async-start | bytes 18874368 | tf_op jit(solution)/shard_map/all_gather | solution.py:41
  12.5 795.0 %reduce-scatter.2.cloned.1.call-start = ((), (), s32[]{:S(2)}) async-start(), calls=%async_computation.4 | async-start | bytes 3932160 | tf_op jit(solution)/shard_map/reduce_scatter | solution.py:44
  12.5 56.7 %collective-permute-start = (bf16[512,2048]{1,0:T(8,128)(2,1)S(1)}, bf16[512,2048]{1,0:T(8,128)(2,1)S(1)}, u32[]{:S(2)}, u32[]{:S(2)}) collective-permute-start(bf16[512,2048]{1,0:T(8,128)(2,1)S(1)} %copy-done.1), channel_id=1, source_target_pairs={{0,4},{4,8},{8,12},{12,16},{16,20},{20,24},{24,28},{28,0},{1,5},{5... | collective-permute-start | bytes 6291464 | tf_op jit(solution)/shard_map/ppermute | solution.py:18
  69.2 1.3 copy-start.4
  69.2 95.0 %collective-permute-start.1 = (bf16[512,2048]{1,0:T(8,128)(2,1)S(1)}, bf16[512,2048]{1,0:T(8,128)(2,1)S(1)}, u32[]{:S(2)}, u32[]{:S(2)}) collective-permute-start(bf16[512,2048]{1,0:T(8,128)(2,1)S(1)} %collective-permute-done), channel_id=1, source_target_pairs={{0,4},{4,8},{8,12},{12,16},{16,20},{20,24},{24,28},{28,0},{1,5},{5... | collective-permute-start | bytes 6291464 | tf_op jit(solution)/shard_map/ppermute | solution.py:18
  164.3 1.3 copy-start.8
  164.3 85.1 %collective-permute-start.2 = (bf16[512,2048]{1,0:T(8,128)(2,1)S(1)}, bf16[512,2048]{1,0:T(8,128)(2,1)S(1)}, u32[]{:S(2)}, u32[]{:S(2)}) collective-permute-start(bf16[512,2048]{1,0:T(8,128)(2,1)S(1)} %collective-permute-done.1), channel_id=1, source_target_pairs={{0,4},{4,8},{8,12},{12,16},{16,20},{20,24},{24,28},{28,0},{1,5},{5... | collective-permute-start | bytes 6291464 | tf_op jit(solution)/shard_map/ppermute | solution.py:18
  249.3 1.4 copy-start.2
  250.7 95.0 %collective-permute-start.3 = (bf16[512,2048]{1,0:T(8,128)(2,1)S(1)}, bf16[512,2048]{1,0:T(8,128)(2,1)S(1)}, u32[]{:S(2)}, u32[]{:S(2)}) collective-permute-start(bf16[512,2048]{1,0:T(8,128)(2,1)S(1)} %collective-permute-done.2), channel_id=1, source_target_pairs={{0,4},{4,8},{8,12},{12,16},{16,20},{20,24},{24,28},{28,0},{1,5},{5... | collective-permute-start | bytes 6291464 | tf_op jit(solution)/shard_map/ppermute | solution.py:18
  345.7 1.3 copy-start.6
  347.0 99.5 %collective-permute-start.4 = (bf16[512,2048]{1,0:T(8,128)(2,1)S(1)}, bf16[512,2048]{1,0:T(8,128)(2,1)}, u32[]{:S(2)}, u32[]{:S(2)}) collective-permute-start(bf16[512,2048]{1,0:T(8,128)(2,1)S(1)} %collective-permute-done.3), channel_id=1, source_target_pairs={{0,4},{4,8},{8,12},{12,16},{16,20},{20,24},{24,28},{28,0},{1,5},{5... | collective-permute-start | bytes 6291464 | tf_op jit(solution)/shard_map/ppermute | solution.py:18
  446.5 85.5 %collective-permute-start.5 = (bf16[512,2048]{1,0:T(8,128)(2,1)}, bf16[512,2048]{1,0:T(8,128)(2,1)}, u32[]{:S(2)}, u32[]{:S(2)}) collective-permute-start(bf16[512,2048]{1,0:T(8,128)(2,1)} %collective-permute-done.4), channel_id=1, source_target_pairs={{0,4},{4,8},{8,12},{12,16},{16,20},{20,24},{24,28},{28,0},{1,5},{5... | collective-permute-start | bytes 6291464 | tf_op jit(solution)/shard_map/ppermute | solution.py:18
  458.8 73.3 %copy-start.5 = (bf16[512,2048]{1,0:T(8,128)(2,1)S(1)}, bf16[512,2048]{1,0:T(8,128)(2,1)}, u32[]{:S(2)}) copy-start(bf16[512,2048]{1,0:T(8,128)(2,1)} %copy-done.4) | copy-start | bytes 6291460
  460.3 73.2 %copy-start.9 = (bf16[512,2048]{1,0:T(8,128)(2,1)S(1)}, bf16[512,2048]{1,0:T(8,128)(2,1)}, u32[]{:S(2)}) copy-start(bf16[512,2048]{1,0:T(8,128)(2,1)} %copy-done.8) | copy-start | bytes 6291460
  532.0 86.2 %collective-permute-start.6 = (bf16[512,2048]{1,0:T(8,128)(2,1)}, bf16[512,2048]{1,0:T(8,128)(2,1)}, u32[]{:S(2)}, u32[]{:S(2)}) collective-permute-start(bf16[512,2048]{1,0:T(8,128)(2,1)} %collective-permute-done.5), channel_id=1, source_target_pairs={{0,4},{4,8},{8,12},{12,16},{16,20},{20,24},{24,28},{28,0},{1,5},{5... | collective-permute-start | bytes 6291464 | tf_op jit(solution)/shard_map/ppermute | solution.py:18
  533.5 4.2 copy-start.3
  535.0 4.3 copy-start.7
  770.7 0.7 copy-start.10
Sparse Core Ops, SparseCore 0:
  11.1 31.2 all-gather.3
  44.5 358.0 all-gather.5
  404.6 339.7 all-gather.7
  770.8 36.6 reduce-scatter.1
